TPU v7x, 256 devices: a whole 4x4x8 slice. The times are simulated.
256 devices in a mesh: leaf: 8 (over x, core), rows: 32 (over z, y).
Axes of the slice: x: 4, y: 4, z: 8, core: 2. Of those that a mesh axis runs over, the one named last changes fastest.
Arguments:
- leaf_inverse: bfloat16 [16384, 2048], P(('leaf', 'rows')), may hold values from -0.125 to 0.125
- leaf_panel: bfloat16 [245760, 2048], P(('leaf', 'rows')), may hold values from -0.0625 to 0.0625
- mid_inverse: bfloat16 [8192, 2048], P(('leaf', 'rows')), may hold values from -0.125 to 0.125
- mid_panel: bfloat16 [122880, 2048], P(('leaf', 'rows')), may hold values from -0.0625 to 0.0625
- top_inverse: bfloat16 [4096, 2048], P(('leaf', 'rows')), may hold values from -0.125 to 0.125
- top_panel: bfloat16 [61440, 2048], P(('leaf', 'rows')), may hold values from -0.0625 to 0.0625
- leaf_rhs: bfloat16 [128, 16384], P(None, ('leaf', 'rows')), may hold values from -6 to 6
- mid_rhs: bfloat16 [128, 8192], P(None, ('leaf', 'rows')), may hold values from -6 to 6
- top_rhs: bfloat16 [128, 4096], P(None, ('leaf', 'rows')), may hold values from -6 to 6
- outer_solution: bfloat16 [128, 61440], P(None, ('leaf', 'rows')), may hold values from -6 to 6
- leaf_targets: int32 [8, 240], replicated, may hold values from -1 to 255, as said below
- mid_targets: int32 [4, 240], replicated, may hold values from -1 to 255, as said below
- front_counts: int32 [14, 2], replicated, may hold values from 128 to 30720, as said below
Outputs:
- leaf_solution: bfloat16 [128, 16384], P(None, ('leaf', 'rows'))
- mid_solution: bfloat16 [128, 8192], P(None, ('leaf', 'rows'))
- top_solution: bfloat16 [128, 4096], P(None, ('leaf', 'rows'))
- top_contribution: bfloat16 [128, 61440], P(None, ('leaf', 'rows'))
Inputs may be any that keep to these rules, and one draw needn't show every extreme that they name: `front_counts`: row f gives a front's live pivot count and live update row count, leaf fronts first, then middle, then top fronts. Both are positive multiples of 128, at most 2048 and 30720; top front 0 has 2048 pivots and 30720 update rows. A child's update blocks never outnumber its parent's live blocks. `leaf_targets`: row c lists, for each update block j of leaf front c below its live update rows / 128, the block of middle front c // 2 that receives it, and -1 for the other j. The listed blocks are strictly increasing and live in the parent: below its pivot count / 128, or from 16 up to that plus its update rows / 128. `mid_targets`: row c lists, for each update block j of middle front c below its live update rows / 128, the block of top front c // 2 that receives it, and -1 for the other j. The listed blocks are strictly increasing and live in the parent, as for leaf_targets.
All inputs are finite; a program needn't handle non-finite values.
Results may differ from a plain program's by a relative error of at most 0.019.
Values may be sent and summed in bfloat16 or wider, within the bound.
A program may use at most 64 MiB of HBM per device.

v0:
```python
import jax
import jax.numpy as jnp
from jax import lax
from jax.sharding import PartitionSpec as P

FRONT_ROWS = 32768
PIVOTS = 2048
UPDATES = 30720


def from_partner(value, axis, stride):
    mask = 2**stride
    pairs = [(source, source ^ mask) for source in range(lax.axis_size(axis))]
    return lax.ppermute(value, axis, pairs)


def share_sections(piece_part, height, within):
    if height == 0:
        return piece_part
    current = piece_part
    for bit_index in range(height):
        partner = from_partner(current, "leaf", bit_index)
        upper_bit = within // (1 << bit_index) % 2
        lower_first = jnp.concatenate([current, partner], axis=1)
        upper_first = jnp.concatenate([partner, current], axis=1)
        current = jnp.where(upper_bit == 0, lower_first, upper_first)
    return current


def total_sections(partials, height, within):
    if height == 0:
        return partials[:, 0]
    current = partials
    for bit_index in reversed(range(height)):
        halves = current.reshape(current.shape[0], 2, current.shape[1] // 2, current.shape[2])
        upper_bit = within // (1 << bit_index) % 2
        keeping = lax.dynamic_index_in_dim(halves, upper_bit, 1, keepdims=False)
        sending = lax.dynamic_index_in_dim(halves, 1 - upper_bit, 1, keepdims=False)
        current = keeping + from_partner(sending.astype(jnp.bfloat16), "leaf", bit_index).astype(
            sending.dtype
        )
    return current[:, 0]


def place_level(height, section, row_index, row_count):
    group_width = 1 << height
    within = section % group_width
    front_index = section // group_width
    member = within * row_count + row_index
    return (group_width, within, front_index, member)


def live_rows(member, length, count):
    return (member * length + jnp.arange(length) < count)[None, :]


def block_onehot(targets, front_index, start_block, slab_blocks):
    target_row = lax.dynamic_index_in_dim(targets, front_index, 0, keepdims=False)
    target_row = lax.dynamic_slice_in_dim(target_row, start_block, slab_blocks)
    return (target_row[:, None] == jnp.arange(FRONT_ROWS // 128)[None, :]).astype(jnp.bfloat16)


def extend_children(update, height, targets, section, row_index, row_count):
    group_width, within, front_index, member = place_level(height, section, row_index, row_count)
    slab = lax.all_to_all(update, "rows", split_axis=0, concat_axis=1, tiled=True)
    narrow = slab.shape[0]
    slab_blocks = slab.shape[1] // 128
    onehot = block_onehot(targets, front_index, within * slab_blocks, slab_blocks)
    spread = jnp.einsum(
        "cjr,jb->cbr",
        slab.reshape(narrow, slab_blocks, 128),
        onehot,
        preferred_element_type=jnp.float32,
    )
    parent_width = 2 * group_width
    flattened = spread.reshape(narrow, FRONT_ROWS)
    pivot_side = flattened[:, :PIVOTS].reshape(narrow, parent_width, row_count, -1)
    update_side = flattened[:, PIVOTS:].reshape(narrow, parent_width, row_count, -1)
    joined = jnp.concatenate([pivot_side, update_side], axis=3).reshape(narrow, parent_width, -1)
    returned = lax.all_to_all(
        joined.astype(jnp.bfloat16), "rows", split_axis=2, concat_axis=0, tiled=True
    ).astype(joined.dtype)
    return total_sections(returned, height + 1, section % parent_width)


def descend_children(full_local, height, targets, section, row_count, pivot_local):
    group_width = 1 << height
    within = section % group_width
    columns_form = lax.all_to_all(full_local, "rows", split_axis=0, concat_axis=1, tiled=True)
    narrow = columns_form.shape[0]
    shared = share_sections(columns_form[:, None, :], height, within)
    parted = shared.reshape(narrow, group_width, row_count, -1)
    parent_full = jnp.concatenate(
        [
            parted[..., :pivot_local].reshape(narrow, PIVOTS),
            parted[..., pivot_local:].reshape(narrow, UPDATES),
        ],
        axis=1,
    )
    child_width = group_width // 2
    child_within = section % child_width
    child_front = section // child_width
    slab_blocks = UPDATES // (child_width * 128)
    onehot = block_onehot(targets, child_front, child_within * slab_blocks, slab_blocks)
    picked = jnp.einsum(
        "cbr,jb->cjr",
        parent_full.reshape(narrow, FRONT_ROWS // 128, 128),
        onehot,
        preferred_element_type=jnp.float32,
    )
    picked = picked.reshape(narrow, slab_blocks * 128).astype(jnp.bfloat16)
    return lax.all_to_all(picked, "rows", split_axis=1, concat_axis=0, tiled=True)


def separate_sums(partials, group_width, height, within):
    shaped = partials.reshape(partials.shape[0], group_width, -1)
    summed = lax.psum_scatter(
        shaped.astype(jnp.bfloat16), "rows", scatter_dimension=2, tiled=True
    ).astype(jnp.float32)
    return total_sections(summed, height, within)


def body(
    leaf_inverse,
    leaf_panel,
    mid_inverse,
    mid_panel,
    top_inverse,
    top_panel,
    leaf_rhs,
    mid_rhs,
    top_rhs,
    outer_solution,
    leaf_targets,
    mid_targets,
    front_counts,
):
    row_count = lax.axis_size("rows")
    leaf_count = lax.axis_size("leaf")
    section = lax.axis_index("leaf")
    row_index = lax.axis_index("rows")
    inverses = (leaf_inverse, mid_inverse, top_inverse)
    panels = (leaf_panel, mid_panel, top_panel)
    sources = (leaf_rhs, mid_rhs, top_rhs)
    targets = (leaf_targets, mid_targets)
    offsets = (0, leaf_count, leaf_count + leaf_count // 2)
    carried = None
    forward = []
    top_contribution = None
    for height in range(3):
        group_width, within, front_index, member = place_level(
            height, section, row_index, row_count
        )
        inverse = inverses[height]
        panel_rows = panels[height]
        pivot_local = inverse.shape[0]
        pivot_live = live_rows(member, pivot_local, front_counts[offsets[height] + front_index, 0])
        update_live = live_rows(
            member, panel_rows.shape[0], front_counts[offsets[height] + front_index, 1]
        )
        source = sources[height].astype(jnp.float32)
        if carried is not None:
            source = source + carried[:, :pivot_local]
        assembled_local = jnp.where(pivot_live, source, 0.0).astype(jnp.bfloat16)
        gathered = lax.all_gather(assembled_local, "rows", axis=1, tiled=True)
        assembled = share_sections(gathered[:, None, :], height, within).reshape(
            gathered.shape[0], PIVOTS
        )
        solved = jnp.einsum("cp,rp->cr", assembled, inverse, preferred_element_type=jnp.float32)
        solved = jnp.where(pivot_live, solved, 0.0).astype(jnp.bfloat16)
        update = -jnp.einsum("cp,rp->cr", assembled, panel_rows, preferred_element_type=jnp.float32)
        if carried is not None:
            update = carried[:, pivot_local:] + update
        update = jnp.where(update_live, update, 0.0).astype(jnp.bfloat16)
        forward.append(solved)
        if height < 2:
            carried = extend_children(
                update, height, targets[height], section, row_index, row_count
            )
        else:
            top_contribution = update
    solutions = [None, None, None]
    given_rows = outer_solution
    for height in (2, 1, 0):
        group_width, within, front_index, member = place_level(
            height, section, row_index, row_count
        )
        inverse = inverses[height]
        panel_rows = panels[height]
        pivot_local = inverse.shape[0]
        pivot_live = live_rows(member, pivot_local, front_counts[offsets[height] + front_index, 0])
        update_live = live_rows(
            member, panel_rows.shape[0], front_counts[offsets[height] + front_index, 1]
        )
        given_rows = jnp.where(update_live, given_rows, jnp.zeros_like(given_rows))
        partials = jnp.dot(forward[height], inverse, preferred_element_type=jnp.float32) - jnp.dot(
            given_rows, panel_rows, preferred_element_type=jnp.float32
        )
        if height == 0:
            solution = separate_sums(partials, group_width, height, within)
        else:
            solution = separate_sums(partials, group_width, height, within)
        solution = jnp.where(pivot_live, solution, 0.0).astype(jnp.bfloat16)
        solutions[height] = solution
        if height > 0:
            full_local = jnp.concatenate([solution, given_rows], axis=1)
            given_rows = descend_children(
                full_local, height, targets[height - 1], section, row_count, pivot_local
            )
    return (solutions[0], solutions[1], solutions[2], top_contribution)


def solution(mesh):
    placed = (
        P(("leaf", "rows"), None),
        P(("leaf", "rows"), None),
        P(("leaf", "rows"), None),
        P(("leaf", "rows"), None),
        P(("leaf", "rows"), None),
        P(("leaf", "rows"), None),
        P(None, ("leaf", "rows")),
        P(None, ("leaf", "rows")),
        P(None, ("leaf", "rows")),
        P(None, ("leaf", "rows")),
        P(),
        P(),
        P(),
    )
    return jax.shard_map(
        body,
        mesh=mesh,
        in_specs=placed,
        out_specs=(
            P(None, ("leaf", "rows")),
            P(None, ("leaf", "rows")),
            P(None, ("leaf", "rows")),
            P(None, ("leaf", "rows")),
        ),
        check_vma=False,
    )
```

profile of v0, /device:TPU:2, one launch (start us, length us, event | category | flops | bytes accessed | tf_op | source)
XLA Modules:
  0.0 1120.8 jit_solution(15445964068958309150)
XLA Ops:
  7.2 1.5 constant_dynamic-slice_fusion.2
  9.9 0.8 select_convert_fusion.1
  10.7 52.8 %all_gather.9 = bf16[128,2048]{0,1:T(8,128)(2,1)S(1)} all-gather(bf16[128,64]{0,1:T(8,128)(2,1)S(1)} %select_convert_fusion.1), channel_id=1, replica_groups=mesh['leaf'=8,'rows'=32] {'rows'}, dimensions={1}, use_global_device_ids=true | all-gather | bytes 540672 | tf_op jit(solution)/shard_map/all_gather | solution.py:165
  64.7 3.3 fusion.5
  68.2 0.8 all_to_all.84
  69.0 6.1 all-to-all-start
  75.8 10.8 all-to-all-done
  88.5 9.6 copy.158
  98.1 16.8 %reshape.243 = bf16[32,2,2048]{2,1,0:T(2,128)(2,1)} reshape(bf16[16384,2,4]{2,1,0:T(2,128)(2,1)} %bitcast.148) | data formatting | bytes 524288
  114.9 3.9 all-to-all-start.1
  118.8 11.5 %all-to-all-done.1 = bf16[32,2,2048]{2,1,0:T(2,128)(2,1)S(1)} async-done(((bf16[32,2,2048]{2,1,0:T(2,128)(2,1)}), bf16[32,2,2048]{2,1,0:T(2,128)(2,1)S(1)}, u32[]{:S(2)}, u32[]{:S(2)}) %all-to-all-start.1) | async-done | bytes 262176 | tf_op jit(solution)/shard_map/all_to_all | solution.py:80
  130.3 19.1 %reshape.244 = bf16[16384,2,4]{2,1,0:T(2,128)(2,1)} reshape(bf16[32,2,2048]{2,1,0:T(2,128)(2,1)S(1)} %all-to-all-done.1) | data formatting | bytes 524288
  149.4 16.5 %copy.159 = bf16[4,2,16384]{2,0,1:T(4,128)(2,1)S(1)} copy(bf16[4,2,16384]{0,1,2:T(2,128)(2,1)} %bitcast.149) | data formatting | bytes 524288 | tf_op jit(solution)/shard_map/all_to_all | solution.py:80
  168.4 47.3 %all_gather.10 = bf16[128,1024]{0,1:T(8,128)(2,1)S(1)} all-gather(bf16[128,32]{0,1:T(8,128)(2,1)S(1)} %fusion.42), channel_id=1, replica_groups=mesh['leaf'=8,'rows'=32] {'rows'}, dimensions={1}, use_global_device_ids=true | all-gather | bytes 270336 | tf_op jit(solution)/shard_map/all_gather | solution.py:165
  217.0 0.8 collective-permute-done.1
  219.4 5.2 all-to-all-start.2
  224.6 0.8 dynamic-slice_bitcast_fusion
  225.4 10.0 all-to-all-done.2
  237.3 6.6 copy.166
  243.9 16.8 %reshape.245 = bf16[32,2,2048]{2,1,0:T(2,128)(2,1)} reshape(bf16[8192,4,4]{2,1,0:T(4,128)(2,1)} %bitcast.150) | data formatting | bytes 524288
  260.7 3.9 all-to-all-start.3
  264.7 12.0 %all-to-all-done.3 = bf16[32,2,2048]{2,1,0:T(2,128)(2,1)S(1)} async-done(((bf16[32,2,2048]{2,1,0:T(2,128)(2,1)}), bf16[32,2,2048]{2,1,0:T(2,128)(2,1)S(1)}, u32[]{:S(2)}, u32[]{:S(2)}) %all-to-all-start.3) | async-done | bytes 262176 | tf_op jit(solution)/shard_map/all_to_all | solution.py:80
  276.7 19.1 %reshape.246 = bf16[8192,4,4]{2,1,0:T(4,128)(2,1)} reshape(bf16[32,2,2048]{2,1,0:T(2,128)(2,1)S(1)} %all-to-all-done.3) | data formatting | bytes 524288
  295.8 10.9 copy.167
  307.4 0.7 copy.201
  308.8 4.5 collective-permute-done.2
  315.4 41.1 %all_gather.11 = bf16[128,512]{0,1:T(8,128)(2,1)S(1)} all-gather(bf16[128,16]{0,1:T(8,128)(2,1)S(1)} %fusion.48), channel_id=1, replica_groups=mesh['leaf'=8,'rows'=32] {'rows'}, dimensions={1}, use_global_device_ids=true | all-gather | bytes 135168 | tf_op jit(solution)/shard_map/all_gather | solution.py:165
  356.6 1.3 collective-permute-done.4
  359.2 1.6 broadcast_select_fusion.1
  360.7 5.8 collective-permute-done.5
  366.5 1.1 maximum_select_fusion.1
  367.6 1.5 fusion.15
  369.2 1.9 fusion
  371.0 1.0 copy.195
  372.0 213.9 %reduce-scatter.4.cloned.1.call-done = bf16[128,4,16]{0,2,1:T(8,128)(2,1)} async-done(((bf16[128,4,512]{0,2,1:T(8,128)(2,1)}), bf16[128,4,16]{0,2,1:T(8,128)(2,1)}) %reduce-scatter.4.cloned.1.call-update) | async-done | bytes 16400 | tf_op jit(solution)/shard_map/reduce_scatter | solution.py:117
  586.0 0.7 convert.30
  587.3 3.2 collective-permute-done.6
  590.6 1.2 collective-permute-done.7
  591.9 0.8 pad_maximum_fusion.3
  592.8 16.7 %all_to_all.111 = bf16[32,4,256]{2,1,0:T(4,128)(2,1)S(1)} all-to-all(bf16[32,4,256]{2,1,0:T(4,128)(2,1)S(1)} %all_to_all.92), channel_id=1, replica_groups=mesh['leaf'=8,'rows'=32] {'rows'}, dimensions={0} | all-to-all | bytes 131072 | tf_op jit(solution)/shard_map/all_to_all | solution.py:89
  609.5 1.3 collective-permute-done.8
  611.6 5.0 collective-permute-done.9
  618.3 0.9 copy.178
  619.5 0.9 fusion.9
  620.6 0.8 copy.180
  621.3 3.8 all-to-all-start.5
  625.2 2.5 fusion.13
  627.7 8.0 all-to-all-done.5
  636.0 1.8 fusion.1
  637.8 1.0 copy.182
  638.8 211.2 %reduce-scatter.6.cloned.1.call-done = bf16[128,2,32]{0,2,1:T(8,128)(2,1)} async-done(((bf16[128,2,1024]{0,2,1:T(8,128)(2,1)}), bf16[128,2,32]{0,2,1:T(8,128)(2,1)}) %reduce-scatter.6.cloned.1.call-update) | async-done | bytes 16400 | tf_op jit(solution)/shard_map/reduce_scatter | solution.py:117
  850.8 1.1 collective-permute-done.10
  852.8 17.4 %all_to_all.112 = bf16[32,4,512]{2,1,0:T(4,128)(2,1)S(1)} all-to-all(bf16[32,4,512]{2,1,0:T(4,128)(2,1)S(1)} %pad_maximum_fusion.2), channel_id=1, replica_groups=mesh['leaf'=8,'rows'=32] {'rows'}, dimensions={0} | all-to-all | bytes 262144 | tf_op jit(solution)/shard_map/all_to_all | solution.py:89
  870.5 1.3 collective-permute-done.11
  873.4 0.9 copy.187
  874.3 4.6 all-to-all-start.7
  879.2 1.7 fusion.11
  880.9 11.5 %all-to-all-done.7 = bf16[4,32,960]{2,0,1:T(4,128)(2,1)} async-done(((bf16[4,32,960]{2,0,1:T(4,128)(2,1)}), bf16[4,32,960]{2,0,1:T(4,128)(2,1)}, u32[]{:S(2)}, u32[]{:S(2)}) %all-to-all-start.7) | async-done | bytes 245792 | tf_op jit(solution)/shard_map/all_to_all | solution.py:112
  892.4 1.7 all_to_all.102
  894.1 1.8 copy.188
  896.0 4.9 fusion.3
  900.9 2.2 fusion.28
  903.1 209.5 %reduce-scatter.8.cloned.1.call-done = bf16[128,1,64]{0,2,1:T(8,128)(2,1)} async-done(((bf16[128,1,2048]{0,2,1:T(8,128)(2,1)}), bf16[128,1,64]{0,2,1:T(8,128)(2,1)}) %reduce-scatter.8.cloned.1.call-update) | async-done | bytes 16400 | tf_op jit(solution)/shard_map/reduce_scatter | solution.py:117
  1112.6 1.4 fusion.40
  (139 shorter events, 24.6 us)
Async XLA Ops:
  7.2 210.7 %copy-start = (bf16[480,2048]{1,0:T(8,128)(2,1)S(1)}, bf16[480,2048]{1,0:T(8,128)(2,1)}, u32[]{:S(2)}) copy-start(bf16[480,2048]{1,0:T(8,128)(2,1)} %param.16) | copy-start | bytes 5898244
  9.3 0.6 copy-start.6
  63.5 5.5 copy-start.1
  64.2 0.6 copy-start.11
  69.0 17.7 %all-to-all-start = ((bf16[32,4,960]{2,1,0:T(4,128)(2,1)}), bf16[32,4,960]{2,1,0:T(4,128)(2,1)S(1)}, u32[]{:S(2)}, u32[]{:S(2)}) async-start(bf16[32,4,960]{2,1,0:T(4,128)(2,1)} %all_to_all.84), calls=%async_computation | async-start | bytes 524288 | tf_op jit(solution)/shard_map/all_to_all | solution.py:65
  114.9 15.4 %all-to-all-start.1 = ((bf16[32,2,2048]{2,1,0:T(2,128)(2,1)}), bf16[32,2,2048]{2,1,0:T(2,128)(2,1)S(1)}, u32[]{:S(2)}, u32[]{:S(2)}) async-start(bf16[32,2,2048]{2,1,0:T(2,128)(2,1)} %reshape.243), calls=%async_computation.1 | async-start | bytes 524288 | tf_op jit(solution)/shard_map/all_to_all | solution.py:80
  165.9 2.5 copy-start.5
  166.9 1.4 collective-permute-start
  215.7 2.1 collective-permute-start.1
  216.9 20.3 %copy-start.9 = (pred[480]{0:T(512)(128)(4,1)}, pred[480]{0:T(512)(128)(4,1)S(1)}, u32[]{:S(2)}) copy-start(pred[480]{0:T(512)(128)(4,1)S(1)} %add_compare_fusion.1) | copy-start | bytes 1444
  219.4 16.0 %all-to-all-start.2 = ((bf16[32,4,480]{2,1,0:T(4,128)(2,1)}), bf16[32,4,480]{2,1,0:T(4,128)(2,1)S(1)}, u32[]{:S(2)}, u32[]{:S(2)}) async-start(bf16[32,4,480]{2,1,0:T(4,128)(2,1)} %all_to_all.88), calls=%async_computation.2 | async-start | bytes 262144 | tf_op jit(solution)/shard_map/all_to_all | solution.py:65
  225.4 10.9 copy-start.8
  260.7 15.9 %all-to-all-start.3 = ((bf16[32,2,2048]{2,1,0:T(2,128)(2,1)}), bf16[32,2,2048]{2,1,0:T(2,128)(2,1)S(1)}, u32[]{:S(2)}, u32[]{:S(2)}) async-start(bf16[32,2,2048]{2,1,0:T(2,128)(2,1)} %reshape.245), calls=%async_computation.3 | async-start | bytes 524288 | tf_op jit(solution)/shard_map/all_to_all | solution.py:80
  264.6 321.4 %reduce-scatter.4.cloned.1.call-start = ((), (), s32[]{:S(2)}) async-start(), calls=%async_computation.11 | async-start | bytes 540672 | tf_op jit(solution)/shard_map/reduce_scatter | solution.py:117
  306.6 8.7 copy-start.13
  307.3 60.3 %copy-start.3 = (bf16[16,2048]{1,0:T(8,128)(2,1)S(1)}, bf16[16,2048]{1,0:T(8,128)(2,1)}, u32[]{:S(2)}) copy-start(bf16[16,2048]{1,0:T(8,128)(2,1)} %param.17) | copy-start | bytes 196612
  308.1 5.2 collective-permute-start.2
  313.3 1.3 collective-permute-start.3
  314.7 0.7 copy-start.2
  356.5 1.4 collective-permute-start.4
  358.0 8.6 collective-permute-start.5
  359.1 8.5 copy-start.14
  586.7 3.8 collective-permute-start.6
  590.5 45.4 %copy-start.10 = (pred[480]{0:T(512)(128)(4,1)S(1)}, pred[480]{0:T(512)(128)(4,1)}, u32[]{:S(2)}) copy-start(pred[480]{0:T(512)(128)(4,1)} %copy-done.9) | copy-start | bytes 1444
  590.5 1.3 collective-permute-start.7
  591.9 45.9 %copy-start.4 = (bf16[128,16]{0,1:T(8,128)(2,1)}, bf16[128,16]{0,1:T(8,128)(2,1)S(1)}, u32[]{:S(2)}) copy-start(bf16[128,16]{0,1:T(8,128)(2,1)S(1)} %fusion.49) | copy-start | bytes 12292
  609.5 1.3 collective-permute-start.8
  610.9 5.6 collective-permute-start.9
  621.3 14.4 %all-to-all-start.5 = ((bf16[4,32,480]{2,0,1:T(4,128)(2,1)}), bf16[4,32,480]{2,0,1:T(4,128)(2,1)S(1)}, u32[]{:S(2)}, u32[]{:S(2)}) async-start(bf16[4,32,480]{2,0,1:T(4,128)(2,1)} %copy.180), calls=%async_computation.6 | async-start | bytes 262144 | tf_op jit(solution)/shard_map/all_to_all | solution.py:112
  625.2 224.8 %reduce-scatter.6.cloned.1.call-start = ((), (), s32[]{:S(2)}) async-start(), calls=%async_computation.12 | async-start | bytes 540672 | tf_op jit(solution)/shard_map/reduce_scatter | solution.py:117
  638.8 240.4 %copy-start.7 = (pred[64]{0:T(512)(128)(4,1)S(1)}, pred[64]{0:T(512)(128)(4,1)}, u32[]{:S(2)}) copy-start(pred[64]{0:T(512)(128)(4,1)} %copy-done.6) | copy-start | bytes 196
  850.7 1.2 collective-permute-start.10
  870.4 1.4 collective-permute-start.11
  871.9 24.1 %copy-start.12 = (pred[960]{0:T(1024)(128)(4,1)S(1)}, pred[960]{0:T(1024)(128)(4,1)}, u32[]{:S(2)}) copy-start(pred[960]{0:T(1024)(128)(4,1)} %copy-done.11) | copy-start | bytes 2884
  874.3 18.1 %all-to-all-start.7 = ((bf16[4,32,960]{2,0,1:T(4,128)(2,1)}), bf16[4,32,960]{2,0,1:T(4,128)(2,1)}, u32[]{:S(2)}, u32[]{:S(2)}) async-start(bf16[4,32,960]{2,0,1:T(4,128)(2,1)} %copy.187), calls=%async_computation.9 | async-start | bytes 524288 | tf_op jit(solution)/shard_map/all_to_all | solution.py:112
  878.9 233.7 %reduce-scatter.8.cloned.1.call-start = ((), (), s32[]{:S(2)}) async-start(), calls=%async_computation.13 | async-start | bytes 540672 | tf_op jit(solution)/shard_map/reduce_scatter | solution.py:117
  880.8 20.1 %copy-start.15 = (pred[240]{0:T(512)(128)(4,1)S(1)}, pred[240]{0:T(512)(128)(4,1)}, u32[]{:S(2)}) copy-start(pred[240]{0:T(512)(128)(4,1)} %copy-done.14) | copy-start | bytes 724
Sparse Core Ops, SparseCore 0:
  372.2 213.7 reduce-scatter.3
  638.9 211.0 reduce-scatter.5
  901.0 211.5 reduce-scatter.7
where the time goes:
time: 1130 us; the launch traced here: 1120 us
  waiting for transfers between devices  725 us (64%)
  blocking collectives  175 us (15%)
  local copies, waits for them, and re-layouts  139 us (12%)
  starting transfers between devices  31.1 us (3%)
  matrix products  22.3 us (2%)
  between operations  14.9 us (1%)
  other arithmetic  13.2 us (1%)
    reduce_scatter x3, waiting for transfers between devices, separate_sums(): lax.psum_scatter(shaped.astype(jnp.bfloat16), 'rows', scatter_dimension=2...  635 us
    all_gather x3, blocking collectives, body(): gathered = lax.all_gather(assembled_local, 'rows', axis=1, tiled=True)  141 us
    unnamed x42, local copies, waits for them, and re-layouts  75.2 us
    all_to_all x2, blocking collectives, descend_children(): lax.all_to_all(full_local, 'rows', split_axis=0, concat_axis=1, tiled=True)  34.1 us
    all_to_all x2, local copies, waits for them, and re-layouts, extend_children(): lax.all_to_all(joined.astype(jnp.bfloat16), 'rows', split_axis=2, concat_...  27.3 us
    ppermute x12, waiting for transfers between devices, from_partner(): return lax.ppermute(value, axis, pairs)  26.3 us
    all_to_all x2, waiting for transfers between devices, extend_children(): lax.all_to_all(joined.astype(jnp.bfloat16), 'rows', split_axis=2, concat_...  23.5 us
  transfers between devices with their start and end apart: 21, of which 21 were waited for; matrix products, arithmetic and copies ran while one was open for 1% of the time, Pallas kernels for 0%

commit v1 on v0

--- a/solution.py
+++ b/solution.py
@@ -77,8 +77,14 @@
     pivot_side = flattened[:, :PIVOTS].reshape(narrow, parent_width, row_count, -1)
     update_side = flattened[:, PIVOTS:].reshape(narrow, parent_width, row_count, -1)
     joined = jnp.concatenate([pivot_side, update_side], axis=3).reshape(narrow, parent_width, -1)
-    returned = lax.all_to_all(
-        joined.astype(jnp.bfloat16), "rows", split_axis=2, concat_axis=0, tiled=True
+    returned = jnp.concatenate(
+        lax.all_to_all(
+            jnp.stack(jnp.split(joined.astype(jnp.bfloat16), lax.axis_size("rows"), axis=2)),
+            "rows",
+            split_axis=0,
+            concat_axis=0,
+        ),
+        axis=0,
     ).astype(joined.dtype)
     return total_sections(returned, height + 1, section % parent_width)
 

time: 1130 us -> 1010 us (0.89)
  waiting for transfers between devices: 725 us -> 653 us
  local copies, waits for them, and re-layouts: 139 us -> 83.8 us
    reduce_scatter x3 -> x2, waiting for transfers between devices: 635 us -> 421 us  [separate_sums(): lax.psum_scatter(shaped.astype(jnp.bfloat16), 'rows', scatter_dimension=2...]
    unnamed x3 -> x4, waiting for transfers between devices: 0.05 us -> 144 us
    unnamed x42 -> x106, local copies, waits for them, and re-layouts: 75.2 us -> 39.4 us
    all_to_all x2 -> x0, local copies, waits for them, and re-layouts: 27.3 us -> none  [extend_children(): lax.all_to_all(joined.astype(jnp.bfloat16), 'rows', split_axis=2, concat_...]
    concatenate x2 -> x0, local copies, waits for them, and re-layouts: 16.2 us -> none  [extend_children(): jnp.concatenate([pivot_side, update_side], axis=3)]
  transfers between devices with their start and end apart: 21 -> 21, of which waited for: 21 -> 21; matrix products, arithmetic and copies ran while one was open for 1% -> 2% of each run, Pallas kernels for 0% -> 0%
where the time goes in v1:
time: 1010 us
  waiting for transfers between devices  653 us (65%)
  blocking collectives  174 us (17%)
  local copies, waits for them, and re-layouts  83.8 us (8%)
  starting transfers between devices  31.5 us (3%)
  matrix products  25 us (2%)
  other arithmetic  22.4 us (2%)
  between operations  15.3 us (2%)
    reduce_scatter x2, waiting for transfers between devices, separate_sums(): lax.psum_scatter(shaped.astype(jnp.bfloat16), 'rows', scatter_dimension=2...  421 us
    unnamed x4, waiting for transfers between devices  144 us
    all_gather x3, blocking collectives, body(): gathered = lax.all_gather(assembled_local, 'rows', axis=1, tiled=True)  141 us
    unnamed x106, local copies, waits for them, and re-layouts  39.4 us
    all_to_all x2, blocking collectives, descend_children(): lax.all_to_all(full_local, 'rows', split_axis=0, concat_axis=1, tiled=True)  33.1 us
    ppermute x12, waiting for transfers between devices, from_partner(): return lax.ppermute(value, axis, pairs)  24.3 us
    all_to_all x2, waiting for transfers between devices, extend_children(): lax.all_to_all(jnp.stack(jnp.split(joined.astype(jnp.bfloat16), lax.axis_...  23.2 us
    all_to_all x2, waiting for transfers between devices, extend_children(): lax.all_to_all(update, 'rows', split_axis=0, concat_axis=1, tiled=True)  20.8 us
  transfers between devices with their start and end apart: 21, of which 21 were waited for; matrix products, arithmetic and copies ran while one was open for 2% of the time, Pallas kernels for 0%

profile of v1, /device:TPU:2, one launch (start us, length us, event | category | flops | bytes accessed | tf_op | source)
XLA Modules:
  0.0 1005.0 jit_solution(10365799077689417231)
XLA Ops:
  7.2 1.6 constant_dynamic-slice_fusion.1
  10.7 52.8 %all_gather.9 = bf16[128,2048]{0,1:T(8,128)(2,1)S(1)} all-gather(bf16[128,64]{0,1:T(8,128)(2,1)S(1)} %select_convert_fusion.1), channel_id=1, replica_groups=mesh['leaf'=8,'rows'=32] {'rows'}, dimensions={1}, use_global_device_ids=true | all-gather | bytes 540672 | tf_op jit(solution)/shard_map/all_gather | solution.py:171
  64.2 3.3 fusion.4
  68.5 6.1 all-to-all-start
  75.3 10.8 %all-to-all-done = bf16[32,4,960]{2,1,0:T(4,128)(2,1)S(1)} async-done(((bf16[32,4,960]{2,1,0:T(4,128)(2,1)}), bf16[32,4,960]{2,1,0:T(4,128)(2,1)S(1)}, u32[]{:S(2)}, u32[]{:S(2)}) %all-to-all-start) | async-done | bytes 245792 | tf_op jit(solution)/shard_map/all_to_all | solution.py:65
  107.4 3.9 all-to-all-start.1
  111.3 11.5 %all-to-all-done.1 = bf16[32,4,2,512]{3,2,1,0:T(2,128)(2,1)S(1)} async-done(((bf16[32,4,2,512]{3,2,1,0:T(2,128)(2,1)}), bf16[32,4,2,512]{3,2,1,0:T(2,128)(2,1)S(1)}, u32[]{:S(2)}, u32[]{:S(2)}) %all-to-all-start.1) | async-done | bytes 262176 | tf_op jit(solution)/shard_map/all_to_all | solution.py:81
  125.0 1.3 convert_add_fusion
  126.5 47.3 %all_gather.10 = bf16[128,1024]{0,1:T(8,128)(2,1)S(1)} all-gather(bf16[128,32]{0,1:T(8,128)(2,1)S(1)} %fusion.41), channel_id=1, replica_groups=mesh['leaf'=8,'rows'=32] {'rows'}, dimensions={1}, use_global_device_ids=true | all-gather | bytes 270336 | tf_op jit(solution)/shard_map/all_gather | solution.py:171
  175.5 1.1 maximum_select_fusion
  178.2 5.2 all-to-all-start.2
  184.1 10.0 all-to-all-done.2
  196.5 1.1 pad_maximum_fusion.1
  217.0 4.6 all-to-all-start.3
  221.9 11.7 %all-to-all-done.3 = bf16[32,4,4,256]{3,2,1,0:T(4,128)(2,1)} async-done(((bf16[32,4,4,256]{3,2,1,0:T(4,128)(2,1)}), bf16[32,4,4,256]{3,2,1,0:T(4,128)(2,1)}, u32[]{:S(2)}, u32[]{:S(2)}) %all-to-all-start.3) | async-done | bytes 262176 | tf_op jit(solution)/shard_map/all_to_all | solution.py:81
  233.5 1.0 copy_convert_fusion
  234.6 1.1 copy.1862
  235.7 1.2 reshape.231
  237.6 1.7 copy.1864
  240.5 1.1 copy.1863
  241.6 2.9 collective-permute-done.2
  247.0 41.2 %all_gather.11 = bf16[128,512]{0,1:T(8,128)(2,1)S(1)} all-gather(bf16[128,16]{0,1:T(8,128)(2,1)S(1)} %fusion.47), channel_id=1, replica_groups=mesh['leaf'=8,'rows'=32] {'rows'}, dimensions={1}, use_global_device_ids=true | all-gather | bytes 135168 | tf_op jit(solution)/shard_map/all_gather | solution.py:171
  288.2 1.3 collective-permute-done.4
  290.9 1.6 broadcast_select_fusion.1
  292.5 5.7 collective-permute-done.5
  298.1 1.4 maximum_select_fusion.1
  299.5 2.4 fusion.14
  302.0 2.7 fusion
  304.6 2.2 convert_element_type.191
  306.9 2.2 copy.1865
  310.3 144.4 %all-reduce.3.cloned.1.call-done = bf16[128,4,512]{0,1,2:T(4,128)(2,1)} async-done(((bf16[128,4,512]{0,1,2:T(4,128)(2,1)}), bf16[128,4,512]{0,1,2:T(4,128)(2,1)}) %all-reduce.3.cloned.1.call-update) | async-done | bytes 524304
  456.1 3.1 collective-permute-done.6
  459.3 1.2 collective-permute-done.7
  461.1 1.5 pad_maximum_fusion.3
  462.6 1.6 copy.1867
  464.2 1.5 all_to_all.84
  465.7 15.5 %all_to_all.103 = bf16[32,4,256]{2,1,0:T(4,128)(2,1)S(1)} all-to-all(bf16[32,4,256]{2,1,0:T(4,128)(2,1)} %all_to_all.84), channel_id=1, replica_groups=mesh['leaf'=8,'rows'=32] {'rows'}, dimensions={0} | all-to-all | bytes 131072 | tf_op jit(solution)/shard_map/all_to_all | solution.py:95
  481.2 1.3 collective-permute-done.8
  483.3 4.9 collective-permute-done.9
  490.1 2.1 reshape.223
  492.3 1.6 copy.1873
  493.8 1.1 reshape.222
  494.9 1.1 maximum_bitcast_fusion
  496.0 1.5 fusion.8
  497.5 1.8 convert_element_type.200
  499.2 1.7 copy.1875
  500.9 4.7 all-to-all-start.5
  505.7 2.5 fusion.12
  508.2 7.9 all-to-all-done.5
  517.9 1.9 fusion.1
  520.8 211.2 %reduce-scatter.3.cloned.1.call-done = bf16[128,2,32]{0,2,1:T(8,128)(2,1)} async-done(((bf16[128,2,1024]{0,2,1:T(8,128)(2,1)}), bf16[128,2,32]{0,2,1:T(8,128)(2,1)}) %reduce-scatter.3.cloned.1.call-update) | async-done | bytes 16400 | tf_op jit(solution)/shard_map/reduce_scatter | solution.py:123
  734.9 17.6 %all_to_all.104 = bf16[32,4,512]{2,1,0:T(4,128)(2,1)S(1)} all-to-all(bf16[32,4,512]{2,1,0:T(4,128)(2,1)S(1)} %pad_maximum_fusion.2), channel_id=1, replica_groups=mesh['leaf'=8,'rows'=32] {'rows'}, dimensions={0} | all-to-all | bytes 262144 | tf_op jit(solution)/shard_map/all_to_all | solution.py:95
  752.5 1.3 collective-permute-done.11
  755.5 2.1 reshape.226
  758.6 1.1 maximum_bitcast_fusion.1
  759.6 1.7 fusion.7
  761.3 1.2 convert_element_type.209
  763.4 3.9 all-to-all-start.7
  767.3 2.2 fusion.10
  769.5 11.3 %all-to-all-done.7 = bf16[4,32,960]{2,0,1:T(4,128)(2,1)S(1)} async-done(((bf16[4,32,960]{2,0,1:T(4,128)(2,1)}), bf16[4,32,960]{2,0,1:T(4,128)(2,1)S(1)}, u32[]{:S(2)}, u32[]{:S(2)}) %all-to-all-start.7) | async-done | bytes 245792 | tf_op jit(solution)/shard_map/all_to_all | solution.py:118
  781.1 3.2 fusion.2
  785.4 2.2 fusion.27
  787.7 209.4 %reduce-scatter.5.cloned.1.call-done = bf16[128,1,64]{0,2,1:T(8,128)(2,1)} async-done(((bf16[128,1,2048]{0,2,1:T(8,128)(2,1)}), bf16[128,1,64]{0,2,1:T(8,128)(2,1)}) %reduce-scatter.5.cloned.1.call-update) | async-done | bytes 16400 | tf_op jit(solution)/shard_map/reduce_scatter | solution.py:123
  997.1 1.4 fusion.39
  (205 shorter events, 75.3 us)
Async XLA Ops:
  7.2 169.5 %copy-start = (bf16[480,2048]{1,0:T(8,128)(2,1)S(1)}, bf16[480,2048]{1,0:T(8,128)(2,1)}, u32[]{:S(2)}) copy-start(bf16[480,2048]{1,0:T(8,128)(2,1)} %param.16) | copy-start | bytes 5898244
  9.4 0.6 copy-start.10
  64.2 4.3 copy-start.15
  68.5 17.7 %all-to-all-start = ((bf16[32,4,960]{2,1,0:T(4,128)(2,1)}), bf16[32,4,960]{2,1,0:T(4,128)(2,1)S(1)}, u32[]{:S(2)}, u32[]{:S(2)}) async-start(bf16[32,4,960]{2,1,0:T(4,128)(2,1)} %all_to_all.76), calls=%async_computation | async-start | bytes 524288 | tf_op jit(solution)/shard_map/all_to_all | solution.py:65
  75.3 11.9 %copy-start.6 = (s32[1,240]{1,0:T(1,128)}, s32[1,240]{1,0:T(1,128)S(1)}, u32[]{:S(2)}) copy-start(s32[1,240]{1,0:T(1,128)S(1)} %constant_dynamic-slice_fusion.3) | copy-start | bytes 2884
  86.2 40.3 %copy-start.7 = (bf16[128,32]{0,1:T(8,128)(2,1)S(1)}, bf16[128,32]{0,1:T(8,128)(2,1)}, u32[]{:S(2)}) copy-start(bf16[128,32]{0,1:T(8,128)(2,1)} %param.20) | copy-start | bytes 24580
  107.4 15.4 %all-to-all-start.1 = ((bf16[32,4,2,512]{3,2,1,0:T(2,128)(2,1)}), bf16[32,4,2,512]{3,2,1,0:T(2,128)(2,1)S(1)}, u32[]{:S(2)}, u32[]{:S(2)}) async-start(bf16[32,4,2,512]{3,2,1,0:T(2,128)(2,1)} %constant_dynamic-update-slice_fusion), calls=%async_computation.1 | async-start | bytes 524288 | tf_op jit(solution)/shard_map/all_to_all | solution.py:81
  123.2 1.8 collective-permute-start
  124.0 71.1 %copy-start.8 = (pred[32]{0:T(512)(128)(4,1)}, pred[32]{0:T(512)(128)(4,1)S(1)}, u32[]{:S(2)}) copy-start(pred[32]{0:T(512)(128)(4,1)S(1)} %add_compare_fusion.4) | copy-start | bytes 100
  173.8 1.7 collective-permute-start.1
  174.6 8.8 copy-start.13
  178.2 16.0 %all-to-all-start.2 = ((bf16[32,4,480]{2,1,0:T(4,128)(2,1)}), bf16[32,4,480]{2,1,0:T(4,128)(2,1)S(1)}, u32[]{:S(2)}, u32[]{:S(2)}) async-start(bf16[32,4,480]{2,1,0:T(4,128)(2,1)} %all_to_all.80), calls=%async_computation.2 | async-start | bytes 262144 | tf_op jit(solution)/shard_map/all_to_all | solution.py:65
  184.1 53.5 %copy-start.12 = (s32[120]{0:T(128)}, s32[120]{0:T(128)S(1)}, u32[]{:S(2)}) copy-start(s32[120]{0:T(128)S(1)} %dynamic-slice_bitcast_fusion) | copy-start | bytes 1444
  196.5 50.4 %copy-start.16 = (bf16[128,16]{0,1:T(8,128)(2,1)S(1)}, bf16[128,16]{0,1:T(8,128)(2,1)}, u32[]{:S(2)}) copy-start(bf16[128,16]{0,1:T(8,128)(2,1)} %param.21) | copy-start | bytes 12292
  217.0 16.6 %all-to-all-start.3 = ((bf16[32,4,4,256]{3,2,1,0:T(4,128)(2,1)}), bf16[32,4,4,256]{3,2,1,0:T(4,128)(2,1)}, u32[]{:S(2)}, u32[]{:S(2)}) async-start(bf16[32,4,4,256]{3,2,1,0:T(4,128)(2,1)} %constant_dynamic-update-slice_fusion.32), calls=%async_computation.3 | async-start | bytes 524288 | tf_op jit(solution)/shard_map/all_to_all | solution.py:81
  221.6 233.1 %all-reduce.3.cloned.1.call-start = ((), (), s32[]{:S(2)}) async-start(), calls=%async_computation.12 | async-start | bytes 1048576
  239.3 5.3 collective-permute-start.2
  245.5 1.3 collective-permute-start.3
  246.9 41.3 %copy-start.3 = (f32[128,256]{0,1:T(8,128)}, f32[128,256]{0,1:T(8,128)S(1)}, u32[]{:S(2)}) copy-start(f32[128,256]{0,1:T(8,128)S(1)} %add_bitcast_fusion) | copy-start | bytes 393220
  288.2 1.4 collective-permute-start.4
  289.6 2.9 copy-start.2
  289.6 8.6 collective-permute-start.5
  290.9 1.6 copy-start.17
  292.5 16.6 %copy-start.19 = (u32[256]{0:T(256)S(1)}, u32[256]{0:T(256)}, u32[]{:S(2)}) copy-start(u32[256]{0:T(256)} %constant.277) | copy-start | bytes 3076
  455.5 3.7 collective-permute-start.6
  459.2 1.2 collective-permute-start.7
  460.5 0.6 copy-start.5
  481.2 1.3 collective-permute-start.8
  482.5 5.6 collective-permute-start.9
  500.9 231.9 %copy-start.14 = (pred[480]{0:T(512)(128)(4,1)S(1)}, pred[480]{0:T(512)(128)(4,1)}, u32[]{:S(2)}) copy-start(pred[480]{0:T(512)(128)(4,1)} %copy-done.13) | copy-start | bytes 1444
  500.9 15.2 %all-to-all-start.5 = ((bf16[4,32,480]{2,0,1:T(4,128)(2,1)}), bf16[4,32,480]{2,0,1:T(4,128)(2,1)}, u32[]{:S(2)}, u32[]{:S(2)}) async-start(bf16[4,32,480]{2,0,1:T(4,128)(2,1)} %copy.1875), calls=%async_computation.5 | async-start | bytes 262144 | tf_op jit(solution)/shard_map/all_to_all | solution.py:118
  505.6 228.3 %copy-start.9 = (pred[32]{0:T(512)(128)(4,1)S(1)}, pred[32]{0:T(512)(128)(4,1)}, u32[]{:S(2)}) copy-start(pred[32]{0:T(512)(128)(4,1)} %copy-done.8) | copy-start | bytes 100
  505.6 226.4 %reduce-scatter.3.cloned.1.call-start = ((), (), s32[]{:S(2)}) async-start(), calls=%async_computation.10 | async-start | bytes 540672 | tf_op jit(solution)/shard_map/reduce_scatter | solution.py:123
  520.8 246.5 %copy-start.1 = (bf16[64,2048]{1,0:T(8,128)(2,1)S(1)}, bf16[64,2048]{1,0:T(8,128)(2,1)}, u32[]{:S(2)}) copy-start(bf16[64,2048]{1,0:T(8,128)(2,1)} %param.13) | copy-start | bytes 786436
  732.8 1.2 collective-permute-start.10
  752.5 1.3 collective-permute-start.11
  763.4 17.4 %all-to-all-start.7 = ((bf16[4,32,960]{2,0,1:T(4,128)(2,1)}), bf16[4,32,960]{2,0,1:T(4,128)(2,1)S(1)}, u32[]{:S(2)}, u32[]{:S(2)}) async-start(bf16[4,32,960]{2,0,1:T(4,128)(2,1)} %copy.1882), calls=%async_computation.8 | async-start | bytes 524288 | tf_op jit(solution)/shard_map/all_to_all | solution.py:118
  767.3 229.9 %reduce-scatter.5.cloned.1.call-start = ((), (), s32[]{:S(2)}) async-start(), calls=%async_computation.11 | async-start | bytes 540672 | tf_op jit(solution)/shard_map/reduce_scatter | solution.py:123
  780.9 4.5 copy-start.4
  780.9 4.5 copy-start.18
  781.1 216.0 %copy-start.11 = (pred[64]{0:T(512)(128)(4,1)S(1)}, pred[64]{0:T(512)(128)(4,1)}, u32[]{:S(2)}) copy-start(pred[64]{0:T(512)(128)(4,1)} %copy-done.10) | copy-start | bytes 196
Sparse Core Ops, SparseCore 0:
  309.2 145.5 all-reduce.2
  521.0 211.0 reduce-scatter.2
  785.5 211.5 reduce-scatter.4
